TPU v7x, 512 devices: a whole 4x8x8 slice. The times are simulated.
512 devices in a mesh: row: 16 (over x_hi, z), col: 32 (over y, x_lo, core).
Axes of the slice: x: 4 (x_hi: 2, x_lo: 2; x = x_hi * 2 + x_lo), y: 8, z: 8, core: 2. Of those that a mesh axis runs over, the one named last changes fastest.
Arguments:
- activations: bfloat16 [1024, 28672], P('row', 'col'), may hold values from -0.1875 to 0.1875
- cotangent: bfloat16 [1024, 16384], P('col', 'row'), may hold values from -6 to 6
- down_weight: bfloat16 [28672, 16384], P('col', 'row'), may hold values from -0.046875 to 0.046875
- row_order: int32 [1024], replicated, may hold values from 0 to 1023, each once
Outputs:
- weight_grad: bfloat16 [28672, 16384], P('col', 'row')
- input_grad: bfloat16 [1024, 28672], P('row', 'col')
Inputs may be any that keep to these rules, and one draw needn't show every extreme that they name: `row_order`: each of the 1024 rows is named exactly once.
All inputs are finite; a program needn't handle non-finite values.
Results may differ from a plain program's by a relative error of at most 0.001.
Values may be sent and summed in bfloat16 or wider, within the bound.
A program may use at most 64 MiB of HBM per device.

v0:
```python
import jax
import jax.numpy as jnp
from jax import lax
from jax.sharding import PartitionSpec as P


def contract_rows(left, right):
    return lax.dot_general(
        left, right, (((0,), (0,)), ((), ())), preferred_element_type=jnp.float32
    )


def contract_cols(left, right):
    return lax.dot_general(
        left, right, (((1,), (1,)), ((), ())), preferred_element_type=jnp.float32
    )


def body(activations, cotangent, down_weight, row_order):
    gathered = lax.all_gather(cotangent, "col", axis=0, tiled=True)
    aligned = jnp.take(gathered, row_order, axis=0)
    all_rows = lax.all_gather(activations, "row", axis=0, tiled=True)
    weight_total = contract_rows(all_rows, aligned)
    weight_grad = weight_total.astype(jnp.bfloat16)
    partial_sums = contract_cols(aligned, down_weight)
    summed = lax.psum_scatter(partial_sums, "row", scatter_dimension=0, tiled=True)
    input_grad = summed.astype(jnp.bfloat16)
    return (weight_grad, input_grad)


def solution(mesh):
    in_specs = (P("row", "col"), P("col", "row"), P("col", "row"), P())
    out_specs = (P("col", "row"), P("row", "col"))
    return jax.shard_map(body, mesh=mesh, in_specs=in_specs, out_specs=out_specs, check_vma=False)
```

profile of v0, /device:TPU:8, one launch (start us, length us, event | category | flops | bytes accessed | tf_op | source)
XLA Modules:
  0.0 402.1 jit_solution(9003948174916197972)
XLA Ops:
  7.2 0.0 copy-start
  7.2 0.0 all-gather.3.cloned.1.call-start
  7.2 0.7 all-gather.3.cloned.1.call-update
  7.9 0.0 all-gather.5.cloned.1.call-start
  8.0 0.7 all-gather.5.cloned.1.call-update
  8.7 0.0 reduce-scatter.2.cloned.1.call-start
  8.7 0.7 compare_and_fusion
  9.4 0.7 fusion.1
  10.1 71.0 %all-gather.3.cloned.1.call-done = bf16[1024,1024]{1,0:T(8,128)(2,1)} async-done(((bf16[32,1024]{1,0:T(8,128)(2,1)}), bf16[1024,1024]{1,0:T(8,128)(2,1)}) %all-gather.3.cloned.1.call-update) | async-done | bytes 2097168 | tf_op jit(solution)/shard_map/all_gather | solution.py:20
  81.1 7.9 %gather_fusion = bf16[1024,1024]{1,0:T(8,128)(2,1)} fusion(bf16[1024,1024]{1,0:T(8,128)(2,1)} %all-gather.3.cloned.1.call-done, s32[1024]{0:T(1024)S(1)} %fusion.1), kind=kCustom, calls=%fused_computation | custom fusion | bytes 4198400 | tf_op jit(solution)/shard_map/jit(_take)/gather | solution.py:21
  89.0 0.0 copy-done
  89.0 5.8 %fusion = f32[1024,896]{1,0:T(8,128)} fusion(bf16[896,1024]{1,0:T(8,128)(2,1)S(1)} %copy-done, bf16[1024,1024]{1,0:T(8,128)(2,1)} %gather_fusion, pred[1024]{0:T(1024)(128)(4,1)S(1)} %compare_and_fusion), kind=kOutput, calls=%fused_computation.3 | convolution fusion | flops 1880096768 | bytes 7603200 | tf_op jit(solution)/shard_map/dot_general | solution.py:14
  94.7 0.0 reduce-scatter.2.cloned.1.call-update
  94.8 80.2 %all-gather.5.cloned.1.call-done = bf16[1024,896]{1,0:T(8,128)(2,1)} async-done(((bf16[64,896]{1,0:T(8,128)(2,1)}), bf16[1024,896]{1,0:T(8,128)(2,1)}) %all-gather.5.cloned.1.call-update) | async-done | bytes 1835024 | tf_op jit(solution)/shard_map/all_gather | solution.py:22
  175.0 5.9 %convert_bitcast_fusion = bf16[896,1024]{0,1:T(8,128)(2,1)} fusion(bf16[1024,896]{1,0:T(8,128)(2,1)} %all-gather.5.cloned.1.call-done, bf16[1024,1024]{1,0:T(8,128)(2,1)} %gather_fusion, pred[1024]{0:T(1024)(128)(4,1)S(1)} %compare_and_fusion), kind=kOutput, calls=%fused_computation.2 | convolution fusion | flops 1881014272 | bytes 5768192 | tf_op jit(solution)/shard_map/dot_general | solution.py:8
  180.9 3.8 copy.6
  184.7 209.3 %reduce-scatter.2.cloned.1.call-done = f32[64,896]{1,0:T(8,128)} async-done(((f32[1024,896]{1,0:T(8,128)}), f32[64,896]{1,0:T(8,128)}) %reduce-scatter.2.cloned.1.call-update) | async-done | bytes 229392 | tf_op jit(solution)/shard_map/reduce_scatter | solution.py:26
  394.0 1.6 convert_element_type.11
Async XLA Ops:
  7.2 81.8 %copy-start = (bf16[896,1024]{1,0:T(8,128)(2,1)S(1)}, bf16[896,1024]{1,0:T(8,128)(2,1)}, u32[]{:S(2)}) copy-start(bf16[896,1024]{1,0:T(8,128)(2,1)} %param.6) | copy-start | bytes 5505028
  7.2 73.9 %all-gather.3.cloned.1.call-start = ((), (), s32[]{:S(2)}) async-start(), calls=%async_computation.1 | async-start | bytes 2162688 | tf_op jit(solution)/shard_map/all_gather | solution.py:20
  7.9 167.1 %all-gather.5.cloned.1.call-start = ((), (), s32[]{:S(2)}) async-start(), calls=%async_computation.2 | async-start | bytes 1949696 | tf_op jit(solution)/shard_map/all_gather | solution.py:22
  8.7 385.3 %reduce-scatter.2.cloned.1.call-start = ((), (), s32[]{:S(2)}) async-start(), calls=%async_computation.3 | async-start | bytes 3899392 | tf_op jit(solution)/shard_map/reduce_scatter | solution.py:26
Sparse Core Ops, SparseCore 0:
  10.2 70.8 all-gather.2
  84.3 90.6 all-gather.4
  179.6 214.3 reduce-scatter.1
where the time goes:
time: 402 us
  waiting for transfers between devices  362 us (90%)
  between operations  13.8 us (3%)
  local copies, waits for them, and re-layouts  11.7 us (3%)
  matrix products  11.7 us (3%)
    reduce_scatter x1, waiting for transfers between devices, body(): lax.psum_scatter(partial_sums, 'row', scatter_dimension=0, tiled=True)  209 us
    all_gather x1, waiting for transfers between devices, body(): all_rows = lax.all_gather(activations, 'row', axis=0, tiled=True)  80.2 us
    all_gather x1, waiting for transfers between devices, body(): gathered = lax.all_gather(cotangent, 'col', axis=0, tiled=True)  71 us
  transfers between devices with their start and end apart: 3, of which 3 were waited for; matrix products, arithmetic and copies ran while one was open for 6% of the time, Pallas kernels for 0%

commit v1 on v0

--- a/solution.py
+++ b/solution.py
@@ -19,7 +19,9 @@
 def body(activations, cotangent, down_weight, row_order):
     gathered = lax.all_gather(cotangent, "col", axis=0, tiled=True)
     aligned = jnp.take(gathered, row_order, axis=0)
-    all_rows = lax.all_gather(activations, "row", axis=0, tiled=True)
+    all_rows = jnp.concatenate(
+        lax.all_to_all(jnp.stack([activations] * lax.axis_size("row")), "row", 0, 0), axis=0
+    )
     weight_total = contract_rows(all_rows, aligned)
     weight_grad = weight_total.astype(jnp.bfloat16)
     partial_sums = contract_cols(aligned, down_weight)

time: 402 us -> 337 us (0.84)
  waiting for transfers between devices: 362 us -> 231 us
  blocking collectives: 0 us -> 66 us
    all_gather x1 -> x0, waiting for transfers between devices: 80.2 us -> none  [body(): all_rows = lax.all_gather(activations, 'row', axis=0, tiled=True)]
    all_to_all x0 -> x1, blocking collectives: none -> 66 us  [body(): lax.all_to_all(jnp.stack([activations] * lax.axis_size('row')), 'row', 0, 0)]
    reduce_scatter x1, waiting for transfers between devices: 209 us -> 158 us  [body(): lax.psum_scatter(partial_sums, 'row', scatter_dimension=0, tiled=True)]
  transfers between devices with their start and end apart: 3 -> 2, of which waited for: 3 -> 2; matrix products, arithmetic and copies ran while one was open for 6% -> 3% of each run, Pallas kernels for 0% -> 0%
where the time goes in v1:
time: 337 us; the launch traced here: 336 us
  waiting for transfers between devices  231 us (69%)
  blocking collectives  66 us (20%)
  between operations  14.1 us (4%)
  local copies, waits for them, and re-layouts  12.8 us (4%)
  matrix products  9.55 us (3%)
    reduce_scatter x1, waiting for transfers between devices, body(): lax.psum_scatter(partial_sums, 'row', scatter_dimension=0, tiled=True)  158 us
    all_gather x1, waiting for transfers between devices, body(): gathered = lax.all_gather(cotangent, 'col', axis=0, tiled=True)  71.7 us
    all_to_all x1, blocking collectives, body(): lax.all_to_all(jnp.stack([activations] * lax.axis_size('row')), 'row', 0, 0)  66 us
    gather x1, local copies, waits for them, and re-layouts, body(): aligned = jnp.take(gathered, row_order, axis=0)  7.91 us
  transfers between devices with their start and end apart: 2, of which 2 were waited for; matrix products, arithmetic and copies ran while one was open for 3% of the time, Pallas kernels for 0%

profile of v1, /device:TPU:8, one launch (start us, length us, event | category | flops | bytes accessed | tf_op | source)
XLA Modules:
  0.0 336.4 jit_solution(3002631359378489140)
XLA Ops:
  7.2 0.0 copy-start
  7.2 0.0 all-gather.2.cloned.1.call-start
  7.2 0.7 all-gather.2.cloned.1.call-update
  7.9 0.0 reduce-scatter.2.cloned.1.call-start
  8.0 0.7 compare_and_fusion
  8.7 0.7 fusion.1
  9.3 71.7 %all-gather.2.cloned.1.call-done = bf16[1024,1024]{1,0:T(8,128)(2,1)} async-done(((bf16[32,1024]{1,0:T(8,128)(2,1)}), bf16[1024,1024]{1,0:T(8,128)(2,1)}) %all-gather.2.cloned.1.call-update) | async-done | bytes 2097168 | tf_op jit(solution)/shard_map/all_gather | solution.py:20
  81.1 7.9 %gather_fusion = bf16[1024,1024]{1,0:T(8,128)(2,1)} fusion(bf16[1024,1024]{1,0:T(8,128)(2,1)} %all-gather.2.cloned.1.call-done, s32[1024]{0:T(1024)S(1)} %fusion.1), kind=kCustom, calls=%fused_computation | custom fusion | bytes 4198400 | tf_op jit(solution)/shard_map/jit(_take)/gather | solution.py:21
  89.0 0.0 copy-done
  89.0 5.8 %fusion = f32[1024,896]{1,0:T(8,128)} fusion(bf16[896,1024]{1,0:T(8,128)(2,1)S(1)} %copy-done, bf16[1024,1024]{1,0:T(8,128)(2,1)} %gather_fusion, pred[1024]{0:T(1024)(128)(4,1)S(1)} %compare_and_fusion), kind=kOutput, calls=%fused_computation.3 | convolution fusion | flops 1880096768 | bytes 7603200 | tf_op jit(solution)/shard_map/dot_general | solution.py:14
  94.8 0.0 copy-start.2
  94.8 0.0 reduce-scatter.2.cloned.1.call-update
  94.8 0.9 copy-done.2
  95.7 0.2 stack.2
  95.9 0.0 copy-start.1
  95.9 66.0 %all_to_all.5 = bf16[16,64,896]{2,1,0:T(8,128)(2,1)S(1)} all-to-all(bf16[16,64,896]{2,1,0:T(8,128)(2,1)S(1)} %stack.2), channel_id=1, replica_groups=mesh['row'=16,'col'=32] {'row'}, dimensions={0} | all-to-all | bytes 3670016 | tf_op jit(solution)/shard_map/all_to_all | solution.py:23
  162.0 0.0 copy-done.1
  162.0 3.8 %convert_bitcast_fusion = bf16[896,1024]{0,1:T(8,128)(2,1)} fusion(bf16[1024,896]{1,0:T(8,128)(2,1)S(1)} %bitcast.5, bf16[1024,1024]{1,0:T(8,128)(2,1)S(1)} %copy-done.1, pred[1024]{0:T(1024)(128)(4,1)S(1)} %compare_and_fusion), kind=kOutput, calls=%fused_computation.2 | convolution fusion | flops 1881014272 | bytes 5768192 | tf_op jit(solution)/shard_map/dot_general | solution.py:8
  165.8 3.8 %copy.6 = bf16[896,1024]{1,0:T(8,128)(2,1)} copy(bf16[896,1024]{0,1:T(8,128)(2,1)} %convert_bitcast_fusion) | data formatting | bytes 3670016
  169.5 158.4 %reduce-scatter.2.cloned.1.call-done = f32[64,896]{1,0:T(8,128)} async-done(((f32[1024,896]{1,0:T(8,128)}), f32[64,896]{1,0:T(8,128)}) %reduce-scatter.2.cloned.1.call-update) | async-done | bytes 229392 | tf_op jit(solution)/shard_map/reduce_scatter | solution.py:28
  327.9 1.6 convert_element_type.11
Async XLA Ops:
  7.2 81.8 %copy-start = (bf16[896,1024]{1,0:T(8,128)(2,1)S(1)}, bf16[896,1024]{1,0:T(8,128)(2,1)}, u32[]{:S(2)}) copy-start(bf16[896,1024]{1,0:T(8,128)(2,1)} %param.6) | copy-start | bytes 5505028
  7.2 73.9 %all-gather.2.cloned.1.call-start = ((), (), s32[]{:S(2)}) async-start(), calls=%async_computation.2 | async-start | bytes 2162688 | tf_op jit(solution)/shard_map/all_gather | solution.py:20
  7.9 320.0 %reduce-scatter.2.cloned.1.call-start = ((), (), s32[]{:S(2)}) async-start(), calls=%async_computation.3 | async-start | bytes 3899392 | tf_op jit(solution)/shard_map/reduce_scatter | solution.py:28
  94.8 0.9 copy-start.2
  95.9 66.0 %copy-start.1 = (bf16[1024,1024]{1,0:T(8,128)(2,1)S(1)}, bf16[1024,1024]{1,0:T(8,128)(2,1)}, u32[]{:S(2)}) copy-start(bf16[1024,1024]{1,0:T(8,128)(2,1)} %gather_fusion) | copy-start | bytes 6291460
Sparse Core Ops, SparseCore 0:
  10.2 70.8 all-gather.1
  94.9 232.9 reduce-scatter.1
